TPU v7x, 256 devices: a whole 4x4x8 slice. The times are simulated.
256 devices in a mesh: dom: 64 (over y, z, core), feat: 4 (over x).
Axes of the slice: x: 4, y: 4, z: 8, core: 2. Of those that a mesh axis runs over, the one named last changes fastest.
Arguments:
- features: bfloat16 [128, 65536], P('feat', 'dom'), may hold values from -6 to 6
- tile_mask: int32 [1536, 6, 128, 128], P('dom'), may hold values 0 or 1
- tile_cols: int32 [1536, 6], P('dom'), may hold values from 0 to 23, as said below
- replicas: int32 [3, 131072], P(None, 'dom'), may hold values from 0 to 1023, as said below
- degree: int32 [65536], P('dom'), may hold values from 12 to 47
- self_one: bfloat16 [128, 256], replicated, may hold values from -0.5 to 0.5
- neigh_one: bfloat16 [128, 256], replicated, may hold values from -2 to 2
- self_two: bfloat16 [256, 256], replicated, may hold values from -0.375 to 0.375
- neigh_two: bfloat16 [256, 256], replicated, may hold values from -1.5 to 1.5
Outputs:
- embed: bfloat16 [256, 65536], P('feat', 'dom')
Inputs may be any that keep to these rules, and one draw needn't show every extreme that they name: replicas[0] never names the mirror's own partition; a partition's mirrors with one master partition have distinct slots 0 to at most 63 and distinct master rows; in every draw some master partition receives exactly 64 mirrors from every other partition. `tile_cols`: the 6 column blocks of one row of blocks are distinct.
All inputs are finite; a program needn't handle non-finite values. No bound on the sum of `tile_mask` on one device may be relied on, other than what follows from the above.
Results may differ from a plain program's by a relative error of at most 0.0027.
The roundings to bfloat16 on the way count: a program that leaves them out, or rounds other values in their place, can miss the bound.
Values may be sent and summed in bfloat16 or wider, within the bound.
A program may use at most 64 MiB of HBM per device.

v0:
```python
import jax
import jax.numpy as jnp
from jax import lax
from jax.sharding import PartitionSpec as P


def aggregate_rows(local_values, masks_bf, column_tiles, tile_size):
    feature_row_block, local_rows = local_values.shape
    tiled = local_values.reshape(feature_row_block, local_rows // tile_size, tile_size)
    selected = jnp.take(tiled, column_tiles, axis=1)
    summed = jnp.einsum("fiku,ikvu->fiv", selected, masks_bf, preferred_element_type=jnp.float32)
    return summed.reshape(feature_row_block, local_rows)


def contract(weights, value_rows):
    return lax.dot_general(
        weights, value_rows, (((0,), (0,)), ((), ())), preferred_element_type=jnp.float32
    )


def mix(inputs, neighbours, w_self, w_neigh):
    feat_count = lax.axis_size("feat")
    out_rows = w_self.shape[1] // feat_count
    whole_in, whole_nb = (
        lax.all_gather(inputs, "feat", axis=0, tiled=True),
        lax.all_gather(neighbours, "feat", axis=0, tiled=True),
    )
    column_start = lax.axis_index("feat") * out_rows
    self_cols = lax.dynamic_slice_in_dim(w_self, column_start, out_rows, 1)
    neigh_cols = lax.dynamic_slice_in_dim(w_neigh, column_start, out_rows, 1)
    result = contract(self_cols, whole_in) + contract(neigh_cols, whole_nb)
    return result


def on_device(
    features, tile_mask, tile_cols, replicas, degree, self_one, neigh_one, self_two, neigh_two
):
    dom_count = lax.axis_size("dom")
    masters = features.shape[1]
    mirrors = replicas.shape[1]
    tile_size = tile_mask.shape[-1]
    capacity = 2 * mirrors // dom_count
    slot_count = dom_count * capacity
    position = replicas[0] * capacity + replicas[1]
    send_index = (
        jnp.full((slot_count,), mirrors, jnp.int32)
        .at[position]
        .set(jnp.arange(mirrors, dtype=jnp.int32))
    )
    send_rows = jnp.full((1, slot_count), masters, jnp.int32).at[0, position].set(replicas[2])
    wanted = lax.all_to_all(send_rows, "dom", split_axis=1, concat_axis=1, tiled=True)[0]
    masks_bf = tile_mask.astype(jnp.bfloat16)
    scale = degree.astype(jnp.float32)[None, :]

    def serve(value_rows):
        padded = jnp.concatenate(
            [value_rows, jnp.zeros((value_rows.shape[0], 1), value_rows.dtype)], axis=1
        )
        return jnp.take(padded, wanted, axis=1)

    def collect(received):
        return jnp.take(received, position, axis=1)

    def combine(partial_sum):
        feature_row_block = partial_sum.shape[0]
        rounded_down = partial_sum[:, masters:].astype(jnp.bfloat16)
        padded = jnp.concatenate(
            [rounded_down, jnp.zeros((feature_row_block, 1), jnp.bfloat16)], axis=1
        )
        outgoing = jnp.take(padded, send_index, axis=1)
        received = lax.all_to_all(outgoing, "dom", split_axis=1, concat_axis=1, tiled=True)
        incoming = (
            jnp.zeros((feature_row_block, masters + 1), jnp.float32)
            .at[:, wanted]
            .add(received.astype(jnp.float32))
        )
        total = partial_sum[:, :masters] + incoming[:, :masters]
        return (total / scale).astype(jnp.bfloat16)

    mirror_in = collect(
        lax.all_to_all(serve(features), "dom", split_axis=1, concat_axis=1, tiled=True)
    )
    local_in = jnp.concatenate([features, mirror_in], axis=1)
    mean_one = combine(aggregate_rows(local_in, masks_bf, tile_cols, tile_size))
    hidden_master = jax.nn.relu(mix(features, mean_one, self_one, neigh_one)).astype(jnp.bfloat16)
    hidden_mirror = collect(
        lax.all_to_all(serve(hidden_master), "dom", split_axis=1, concat_axis=1, tiled=True)
    )
    local_hidden = jnp.concatenate([hidden_master, hidden_mirror], axis=1)
    mean_two = combine(aggregate_rows(local_hidden, masks_bf, tile_cols, tile_size))
    return mix(hidden_master, mean_two, self_two, neigh_two).astype(jnp.bfloat16)


def solution(mesh):
    return jax.shard_map(
        on_device,
        mesh=mesh,
        in_specs=(
            P("feat", "dom"),
            P("dom", None, None, None),
            P("dom", None),
            P(None, "dom"),
            P("dom"),
            P(),
            P(),
            P(),
            P(),
        ),
        out_specs=P("feat", "dom"),
        check_vma=False,
    )
```

profile of v0, /device:TPU:1, one launch (start us, length us, event | category | flops | bytes accessed | tf_op | source)
XLA Modules:
  0.0 301.5 jit_solution(11474689041175359031)
XLA Ops:
  3.2 8.1 %scatter_custom_fusion.3 = s32[4096]{0:T(1024)S(1)} fusion(s32[2048]{0:T(1024)S(1)} %broadcast_select_fusion.4, s32[2048]{0:T(1024)S(1)} %bitcast.106, s32[]{:T(128)} %constant.95.clone.1), kind=kCustom, calls=%fused_computation.74 | custom fusion | bytes 16388
  11.9 13.2 %all-to-all-start = ((s32[1,64,64]{2,0,1:T(1,128)}), s32[1,64,64]{2,0,1:T(1,128)S(1)}, u32[]{:S(2)}, u32[]{:S(2)}) async-start(s32[1,64,64]{2,0,1:T(1,128)} %all_to_all.26), calls=%async_computation | async-start | bytes 65536 | tf_op jit(solution)/shard_map/all_to_all | solution.py:51
  25.8 8.1 %scatter_custom_fusion = s32[4096]{0:T(1024)S(1)} fusion(s32[2048]{0:T(1024)S(1)} %bitcast.100, s32[2048]{0:T(1024)S(1)} %iota.3, s32[]{:T(128)} %constant.106.clone.1), kind=kCustom, calls=%fused_computation.76 | custom fusion | bytes 16388 | tf_op jit(solution)/shard_map/scatter | solution.py:48
  37.4 12.1 %gather_fusion = bf16[4096,32]{1,0:T(8,128)(2,1)S(1)} fusion(bf16[32,1025]{0,1:T(8,128)(2,1)S(1)} %concatenate.22, s32[4096]{0:T(1024)S(1)} %broadcast_clamp_fusion), kind=kCustom, calls=%fused_computation | custom fusion | bytes 540672 | tf_op jit(solution)/shard_map/jit(_take)/gather | solution.py:59
  51.0 10.3 %all-to-all-start.1 = ((bf16[64,2,1024]{2,1,0:T(2,128)(2,1)}), bf16[64,2,1024]{2,1,0:T(2,128)(2,1)S(1)}, u32[]{:S(2)}, u32[]{:S(2)}) async-start(bf16[64,2,1024]{2,1,0:T(2,128)(2,1)} %reshape.268), calls=%async_computation.1 | async-start | bytes 524288 | tf_op jit(solution)/shard_map/all_to_all | solution.py:81
  61.4 12.0 %all-to-all-done.1 = bf16[64,2,1024]{2,1,0:T(2,128)(2,1)S(1)} async-done(((bf16[64,2,1024]{2,1,0:T(2,128)(2,1)}), bf16[64,2,1024]{2,1,0:T(2,128)(2,1)S(1)}, u32[]{:S(2)}, u32[]{:S(2)}) %all-to-all-start.1) | async-done | bytes 262176 | tf_op jit(solution)/shard_map/all_to_all | solution.py:81
  74.2 6.2 %gather_fusion.1 = bf16[2048,32]{1,0:T(8,128)(2,1)S(1)} fusion(bf16[32,4096]{0,1:T(8,128)(2,1)S(1)} %bitcast.86, s32[2048]{0:T(1024)S(1)} %broadcast_clamp_fusion.1), kind=kCustom, calls=%fused_computation.1 | custom fusion | bytes 270336 | tf_op jit(solution)/shard_map/jit(_take)/gather | solution.py:62
  87.7 12.1 %gather_fusion.3 = bf16[4096,32]{1,0:T(8,128)(2,1)S(1)} fusion(bf16[32,2049]{0,1:T(8,128)(2,1)S(1)} %concatenate.24.clone, s32[4096]{0:T(1024)S(1)} %fusion.38), kind=kCustom, calls=%fused_computation.3 | custom fusion | bytes 540672 | tf_op jit(solution)/shard_map/jit(_take)/gather | solution.py:70
  101.3 6.0 %all-to-all-start.2 = ((bf16[64,2,1024]{2,1,0:T(2,128)(2,1)}), bf16[64,2,1024]{2,1,0:T(2,128)(2,1)S(1)}, u32[]{:S(2)}, u32[]{:S(2)}) async-start(bf16[64,2,1024]{2,1,0:T(2,128)(2,1)} %reshape.270), calls=%async_computation.2 | async-start | bytes 524288 | tf_op jit(solution)/shard_map/all_to_all | solution.py:71
  107.4 10.8 %all_gather.12 = bf16[128,1024]{1,0:T(8,128)(2,1)S(1)} all-gather(bf16[32,1024]{1,0:T(8,128)(2,1)S(1)} %copy-done.1), channel_id=1, replica_groups=mesh['dom'=64,'feat'=4] {'feat'}, dimensions={0}, use_global_device_ids=true | all-gather | bytes 327680 | tf_op jit(solution)/shard_map/all_gather | solution.py:25
  120.8 24.2 %scatter_custom_fusion.1 = f32[32,1025]{0,1:T(8,128)S(1)} fusion(s32[4096]{0:T(1024)S(1)} %bitcast.103, f32[4096,32]{1,0:T(8,128)S(1)} %copy.107, f32[]{:T(128)} %constant.105.clone.1), kind=kCustom, calls=%fused_computation.47 | custom fusion | flops 131072 | bytes 131204 | tf_op jit(solution)/shard_map/scatter-add | solution.py:75
  145.3 10.3 %all_gather.13 = bf16[128,1024]{1,0:T(8,128)(2,1)S(1)} all-gather(bf16[32,1024]{1,0:T(8,128)(2,1)S(1)} %fusion.30), channel_id=1, replica_groups=mesh['dom'=64,'feat'=4] {'feat'}, dimensions={0}, use_global_device_ids=true | all-gather | bytes 327680 | tf_op jit(solution)/shard_map/all_gather | solution.py:26
  156.2 12.1 %gather_fusion.4 = bf16[4096,64]{1,0:T(8,128)(2,1)S(1)} fusion(bf16[64,1025]{0,1:T(8,128)(2,1)S(1)} %concatenate.25.clone, s32[4096]{0:T(1024)S(1)} %broadcast_clamp_fusion), kind=kCustom, calls=%fused_computation.4 | custom fusion | bytes 1064960 | tf_op jit(solution)/shard_map/jit(_take)/gather | solution.py:59
  169.8 30.6 %all_to_all.39 = bf16[64,2,2048]{2,1,0:T(2,128)(2,1)S(1)} all-to-all(bf16[64,2,2048]{2,1,0:T(2,128)(2,1)S(1)} %reshape.272), channel_id=1, replica_groups=mesh['dom'=64,'feat'=4] {'dom'}, dimensions={0} | all-to-all | bytes 1048576 | tf_op jit(solution)/shard_map/all_to_all | solution.py:87
  201.1 6.2 %gather_fusion.5 = bf16[2048,64]{1,0:T(8,128)(2,1)S(1)} fusion(bf16[64,4096]{0,1:T(8,128)(2,1)S(1)} %bitcast.83, s32[2048]{0:T(1024)S(1)} %broadcast_clamp_fusion.1), kind=kCustom, calls=%fused_computation.5 | custom fusion | bytes 532480 | tf_op jit(solution)/shard_map/jit(_take)/gather | solution.py:62
  207.8 7.5 %gather_fusion.6 = bf16[144,64,128]{1,2,0:T(8,128)(2,1)} fusion(bf16[64,24,128]{0,2,1:T(8,128)(2,1)S(1)} %bitcast.82, s32[1024]{0:T(1024)S(1)} %pad_clamp_fusion), kind=kCustom, calls=%fused_computation.6 | custom fusion | bytes 4719168 | tf_op jit(solution)/shard_map/jit(_take)/gather | solution.py:10
  215.3 5.4 %copy.112 = bf16[144,64,128]{2,1,0:T(8,128)(2,1)S(1)} copy(bf16[144,64,128]{1,2,0:T(8,128)(2,1)} %gather_fusion.6) | data formatting | bytes 4718592 | tf_op jit(solution)/shard_map/jit(_take)/gather | solution.py:10
  220.7 5.5 %fusion.8 = f32[24,8,8,128]{3,2,1,0:T(8,128)S(1)} fusion(s32[24,6,128,128]{3,2,1,0:T(8,128)} %param.10, bf16[24,6,64,128]{3,2,1,0:T(8,128)(2,1)S(1)} %bitcast.84, pred[24,6]{1,0:T(8,128)(4,1)S(1)} %copy.96), kind=kOutput, calls=%fused_computation.21 | convolution fusion | flops 305528832 | bytes 12583056 | tf_op jit(solution)/shard_map/fiku,ikvu->fiv/dot_general | solution.py:11
  226.7 12.1 %gather_fusion.7 = bf16[4096,64]{1,0:T(8,128)(2,1)S(1)} fusion(bf16[64,2049]{0,1:T(8,128)(2,1)S(1)} %concatenate.27.clone, s32[4096]{0:T(1024)S(1)} %fusion.38), kind=kCustom, calls=%fused_computation.7 | custom fusion | bytes 1064960 | tf_op jit(solution)/shard_map/jit(_take)/gather | solution.py:70
  241.1 6.3 %all-to-all-start.4 = ((bf16[64,2,2048]{2,1,0:T(2,128)(2,1)}), bf16[64,2,2048]{2,1,0:T(2,128)(2,1)S(1)}, u32[]{:S(2)}, u32[]{:S(2)}) async-start(bf16[64,2,2048]{2,1,0:T(2,128)(2,1)} %reshape.274), calls=%async_computation.4 | async-start | bytes 1048576 | tf_op jit(solution)/shard_map/all_to_all | solution.py:71
  247.4 10.9 %all_gather.14 = bf16[256,1024]{1,0:T(8,128)(2,1)S(1)} all-gather(bf16[64,1024]{1,0:T(8,128)(2,1)S(1)} %fusion.21), channel_id=1, replica_groups=mesh['dom'=64,'feat'=4] {'feat'}, dimensions={0}, use_global_device_ids=true | all-gather | bytes 655360 | tf_op jit(solution)/shard_map/all_gather | solution.py:25
  258.8 5.9 %all-to-all-done.4 = bf16[64,2,2048]{2,1,0:T(2,128)(2,1)S(1)} async-done(((bf16[64,2,2048]{2,1,0:T(2,128)(2,1)}), bf16[64,2,2048]{2,1,0:T(2,128)(2,1)S(1)}, u32[]{:S(2)}, u32[]{:S(2)}) %all-to-all-start.4) | async-done | bytes 524320 | tf_op jit(solution)/shard_map/all_to_all | solution.py:71
  265.4 24.3 %scatter_custom_fusion.2 = f32[64,1025]{0,1:T(8,128)S(1)} fusion(s32[4096]{0:T(1024)S(1)} %bitcast.104, bf16[64,4096]{0,1:T(8,128)(2,1)S(1)} %bitcast.87, f32[]{:T(128)} %constant.105.clone.1), kind=kCustom, calls=%fused_computation.20 | custom fusion | flops 524288 | bytes 1310980 | tf_op jit(solution)/shard_map/scatter-add | solution.py:75
  290.0 10.5 %all_gather.15 = bf16[256,1024]{1,0:T(8,128)(2,1)S(1)} all-gather(bf16[64,1024]{1,0:T(8,128)(2,1)S(1)} %copy.116), channel_id=1, replica_groups=mesh['dom'=64,'feat'=4] {'feat'}, dimensions={0}, use_global_device_ids=true | all-gather | bytes 655360 | tf_op jit(solution)/shard_map/all_gather | solution.py:26
  (87 shorter events, 30.3 us)
Async XLA Ops:
  0.0 258.2 %copy-start = (bf16[256,256]{1,0:T(8,128)(2,1)S(1)}, bf16[256,256]{1,0:T(8,128)(2,1)}, u32[]{:S(2)}) copy-start(bf16[256,256]{1,0:T(8,128)(2,1)} %param.16) | copy-start | bytes 393220
  11.9 24.1 %all-to-all-start = ((s32[1,64,64]{2,0,1:T(1,128)}), s32[1,64,64]{2,0,1:T(1,128)S(1)}, u32[]{:S(2)}, u32[]{:S(2)}) async-start(s32[1,64,64]{2,0,1:T(1,128)} %all_to_all.26), calls=%async_computation | async-start | bytes 65536 | tf_op jit(solution)/shard_map/all_to_all | solution.py:51
  51.0 22.3 %all-to-all-start.1 = ((bf16[64,2,1024]{2,1,0:T(2,128)(2,1)}), bf16[64,2,1024]{2,1,0:T(2,128)(2,1)S(1)}, u32[]{:S(2)}, u32[]{:S(2)}) async-start(bf16[64,2,1024]{2,1,0:T(2,128)(2,1)} %reshape.268), calls=%async_computation.1 | async-start | bytes 524288 | tf_op jit(solution)/shard_map/all_to_all | solution.py:81
  73.7 7.2 %copy-start.1 = (bf16[32,1024]{1,0:T(8,128)(2,1)S(1)}, bf16[32,1024]{1,0:T(8,128)(2,1)}, u32[]{:S(2)}) copy-start(bf16[32,1024]{1,0:T(8,128)(2,1)} %param.9) | copy-start | bytes 196612
  99.8 7.6 %copy-start.5 = (s32[1024]{0:T(1024)S(1)}, s32[1024]{0:T(1024)}, u32[]{:S(2)}) copy-start(s32[1024]{0:T(1024)} %param.13) | copy-start | bytes 12292
  99.8 18.4 %copy-start.3 = (bf16[128,256]{1,0:T(8,128)(2,1)S(1)}, bf16[128,256]{1,0:T(8,128)(2,1)}, u32[]{:S(2)}) copy-start(bf16[128,256]{1,0:T(8,128)(2,1)} %param.14) | copy-start | bytes 196612
  101.3 18.0 %all-to-all-start.2 = ((bf16[64,2,1024]{2,1,0:T(2,128)(2,1)}), bf16[64,2,1024]{2,1,0:T(2,128)(2,1)S(1)}, u32[]{:S(2)}, u32[]{:S(2)}) async-start(bf16[64,2,1024]{2,1,0:T(2,128)(2,1)} %reshape.270), calls=%async_computation.2 | async-start | bytes 524288 | tf_op jit(solution)/shard_map/all_to_all | solution.py:71
  145.1 10.6 %copy-start.4 = (bf16[128,256]{1,0:T(8,128)(2,1)S(1)}, bf16[128,256]{1,0:T(8,128)(2,1)}, u32[]{:S(2)}) copy-start(bf16[128,256]{1,0:T(8,128)(2,1)} %param.15) | copy-start | bytes 196612
  241.1 23.6 %all-to-all-start.4 = ((bf16[64,2,2048]{2,1,0:T(2,128)(2,1)}), bf16[64,2,2048]{2,1,0:T(2,128)(2,1)S(1)}, u32[]{:S(2)}, u32[]{:S(2)}) async-start(bf16[64,2,2048]{2,1,0:T(2,128)(2,1)} %reshape.274), calls=%async_computation.4 | async-start | bytes 1048576 | tf_op jit(solution)/shard_map/all_to_all | solution.py:71
  265.4 35.2 %copy-start.2 = (bf16[256,256]{1,0:T(8,128)(2,1)S(1)}, bf16[256,256]{1,0:T(8,128)(2,1)}, u32[]{:S(2)}) copy-start(bf16[256,256]{1,0:T(8,128)(2,1)} %param.17) | copy-start | bytes 393220
where the time goes:
time: 303 us; the launch traced here: 302 us
  local copies, waits for them, and re-layouts  105 us (35%)
  blocking collectives  73.1 us (24%)
  other arithmetic  55.8 us (18%)
  starting transfers between devices  35.8 us (12%)
  waiting for transfers between devices  18.8 us (6%)
  matrix products  12.7 us (4%)
    scatter-add x2, other arithmetic, combine(): incoming = jnp.zeros((feature_row_block, masters + 1), jnp.float32).at[:,...  48.5 us
    all_to_all x1, blocking collectives, on_device(): lax.all_to_all(serve(hidden_master), 'dom', split_axis=1, concat_axis=1,...  30.6 us
    gather x3, local copies, waits for them, and re-layouts, combine(): outgoing = jnp.take(padded, send_index, axis=1)  24.7 us
    gather x3, local copies, waits for them, and re-layouts, serve(): return jnp.take(padded, wanted, axis=1)  24.6 us
    all_gather x2, blocking collectives, mix(): lax.all_gather(inputs, 'feat', axis=0, tiled=True)  21.7 us
    all_gather x2, blocking collectives, mix(): lax.all_gather(neighbours, 'feat', axis=0, tiled=True)  20.8 us
    unnamed x26, local copies, waits for them, and re-layouts  16.3 us
    gather x3, local copies, waits for them, and re-layouts, aggregate_rows(): selected = jnp.take(tiled, column_tiles, axis=1)  13.7 us
  transfers between devices with their start and end apart: 4, of which 3 were waited for; matrix products, arithmetic and copies ran while one was open for 4% of the time, Pallas kernels for 0%

commit v1 on v0

v1 whole, which is shorter than its diff:
```python
import jax
import jax.numpy as jnp
from jax import lax
from jax.experimental import pallas as pl
from jax.experimental.pallas import tpu as pltpu
from jax.sharding import PartitionSpec as P

F32, BF16, I32 = jnp.float32, jnp.bfloat16, jnp.int32
MESH = pl.DeviceIdType.MESH
LANES = 128
LO = 256
NN = (((1,), (0,)), ((), ()))
NT = (((1,), (1,)), ((), ()))


def dot(a, b, dims=NN):
    return lax.dot_general(a, b, dims, preferred_element_type=F32)


def kernel(
    doms, feats, cap,
    feat_ref, mask_ref, cols_ref, reps_ref, deg_ref, s1_ref, n1_ref, s2_ref, n2_ref,
    out_ref,
    stage, adj, gate_a, pick_a, gate_b, pick_b, want_out, want_in, whi,
    w1, w2, stacked, unfolded, local, own, mirror_part,
    total, hid, agg1, agg2, feat_all, hid_all, agg1_all, agg2_all,
    box_f1, box_r1, box_f2, box_r2, got_f1, got_r1, got_f2, got_r2,
    mask_sem, send_sem, recv_sem, feat_send, feat_recv,
):
    me, part = lax.axis_index("dom"), lax.axis_index("feat")
    blocks, per_row = cols_ref.shape
    tile = mask_ref.shape[-1]
    masters, mirrors = feat_ref.shape[1], reps_ref.shape[1]
    groups = doms * cap // LO
    each = LO // cap
    quarters = masters // LO
    master_blocks = masters // tile
    low = lax.broadcasted_iota(I32, (1, LANES), 1) < cap

    for i in range(blocks):
        pltpu.make_async_copy(mask_ref.at[i], stage.at[i], mask_sem.at[i]).start()

    barrier = pltpu.get_barrier_semaphore()

    def greet(d, _):
        pl.semaphore_signal(
            barrier, 1, device_id={"dom": lax.rem(me + d, doms)}, device_id_type=MESH
        )
        return 0

    lax.fori_loop(1, doms, greet, 0)
    for d in range(1, feats):
        pl.semaphore_signal(
            barrier, 1, device_id={"feat": lax.rem(part + d, feats)}, device_id_type=MESH
        )

    position = reps_ref[0:1, :] * cap + reps_ref[1:2, :]
    slot_group, slot_column = position >> 8, position & (LO - 1)
    for j in range(0, mirrors, LO):
        rows = lax.broadcasted_iota(I32, (LO, LO), 0)
        hit = rows == slot_column[:, j : j + LO]
        pick_b[:, j : j + LO] = jnp.where(hit, 1.0, 0.0).astype(BF16)
    for h in range(groups):
        hit = jnp.where(slot_group == h, 1.0, 0.0)
        gate_b[h] = jnp.broadcast_to(hit, (16, mirrors)).astype(BF16)

    row = reps_ref[2:3, :]
    kind = lax.broadcasted_iota(I32, (16, 1), 0)
    words = jnp.where(kind == 0, row & (LO - 1), jnp.where(kind == 1, (row >> 8) + 1, 0))
    words = words.astype(F32).astype(BF16)

    def name_rows(h, _):
        slots = dot(words * gate_b[h], pick_b[...], NT)
        value = slots[1:2] * float(LO) + slots[0:1]
        for c in range(LO // LANES):
            pair = value[:, c * LANES : (c + 1) * LANES]
            swapped = pltpu.roll(pair, cap, 1)
            want_out[each * h + 2 * c] = jnp.where(low, pair, 0.0)
            want_out[each * h + 2 * c + 1] = jnp.where(low, swapped, 0.0)
        return 0

    lax.fori_loop(0, groups, name_rows, 0)
    want_in[me] = jnp.zeros((1, LANES), F32)

    pl.semaphore_wait(barrier, doms - 1 + feats - 1)

    def send(box, got, which, q):
        @pl.when(q != me)
        def _():
            pltpu.make_async_remote_copy(
                src_ref=box.at[q],
                dst_ref=got.at[me],
                send_sem=send_sem.at[which],
                recv_sem=recv_sem.at[which],
                device_id={"dom": q},
                device_id_type=MESH,
            ).start()

    def arrived(got, which):
        rest = got.at[pl.ds(0, doms - 1)]
        pltpu.make_async_copy(rest, rest, recv_sem.at[which]).wait()

    def sent(box, which):
        rest = box.at[pl.ds(0, doms - 1)]
        pltpu.make_async_copy(rest, rest, send_sem.at[which]).wait()

    def share(mine, everyone, which):
        everyone[part] = mine[...]
        for d in range(1, feats):
            pltpu.make_async_remote_copy(
                src_ref=mine,
                dst_ref=everyone.at[part],
                send_sem=feat_send.at[which],
                recv_sem=feat_recv.at[which],
                device_id={"feat": lax.rem(part + d, feats)},
                device_id_type=MESH,
            ).start()

    def shared(everyone, which):
        rest = everyone.at[pl.ds(0, feats - 1)]
        pltpu.make_async_copy(rest, rest, feat_recv.at[which]).wait()

    def all_sent(everyone, which):
        rest = everyone.at[pl.ds(0, feats - 1)]
        pltpu.make_async_copy(rest, rest, feat_send.at[which]).wait()

    def ask(d, _):
        send(want_out, want_in, 0, lax.rem(me + d, doms))
        return 0

    lax.fori_loop(1, doms, ask, 0)
    share(feat_ref, feat_all, 0)

    width = w1.shape[0]
    column = lax.broadcasted_iota(I32, (width, s1_ref.shape[1]), 1)
    wanted = lax.broadcasted_iota(I32, column.shape, 0) + part * width
    choose = jnp.where(column == wanted, 1.0, 0.0).astype(BF16)
    fin, hdim = s1_ref.shape[0], s2_ref.shape[0]
    w1[:, :fin] = dot(choose, s1_ref[...], NT).astype(BF16)
    w1[:, fin:] = dot(choose, n1_ref[...], NT).astype(BF16)
    w2[:, :hdim] = dot(choose, s2_ref[...], NT).astype(BF16)
    w2[:, hdim:] = dot(choose, n2_ref[...], NT).astype(BF16)


    arrived(want_in, 0)

    def read_wants(g, _):
        parts = []
        for c in range(LO // LANES):
            even = want_in[each * g + 2 * c]
            odd = pltpu.roll(want_in[each * g + 2 * c + 1], cap, 1)
            parts.append(jnp.where(low, even, odd))
        value = jnp.concatenate(parts, axis=1).astype(I32)
        hit = lax.broadcasted_iota(I32, (LO, LO), 0) == (value & (LO - 1))
        pick_a[g] = jnp.where(hit, 1.0, 0.0).astype(BF16)
        quarter = value >> 8
        whi[g] = quarter
        for h in range(quarters):
            mine = jnp.where(quarter == h + 1, 1.0, 0.0)
            gate_a[g, h] = jnp.broadcast_to(mine, (16, LO)).astype(BF16)
        return 0

    lax.fori_loop(0, groups, read_wants, 0)

    def fold_and_send(values, box, got, which, g, n):
        half = n // 2
        for c in range(LO // LANES):
            pair = values[:, c * LANES : (c + 1) * LANES]
            top, bottom = pair[:half], pltpu.roll(pair[half:], cap, 1)
            even = jnp.where(low, top, bottom)
            odd = pltpu.roll(jnp.where(low, bottom, top), cap, 1)
            box[each * g + 2 * c] = even.astype(BF16)
            box[each * g + 2 * c + 1] = odd.astype(BF16)
        for i in range(each):
            send(box, got, which, each * g + lax.rem(me + i, each))

    def unfold(got, g):
        tops, bottoms = [], []
        for c in range(LO // LANES):
            even = got[each * g + 2 * c].astype(F32)
            odd = pltpu.roll(got[each * g + 2 * c + 1].astype(F32), cap, 1)
            tops.append(jnp.where(low, even, odd))
            bottoms.append(pltpu.roll(jnp.where(low, odd, even), cap, 1))
        top, bottom = jnp.concatenate(tops, axis=1), jnp.concatenate(bottoms, axis=1)
        return jnp.concatenate([top, bottom], axis=0).astype(BF16)

    def serve(values, n, box, got, which):
        got[me] = jnp.zeros(got.shape[1:], BF16)
        for h in range(quarters):
            stacked[pl.ds(h * n, n), :] = values[:, h * LO : (h + 1) * LO]

        def one(d, _):
            g = lax.rem(me // each + d, groups)
            found = dot(stacked[pl.ds(0, quarters * n), :], pick_a[g])
            quarter = whi[g]
            answer = jnp.zeros((n, LO), F32)
            for h in range(quarters):
                answer = jnp.where(quarter == h + 1, found[h * n : (h + 1) * n], answer)
            fold_and_send(answer, box, got, which, g, n)
            return 0

        lax.fori_loop(0, groups, one, 0)

    def place(values, got, which, n):
        for b in range(master_blocks):
            local[b, pl.ds(0, n), :] = values[:, b * tile : (b + 1) * tile]
        arrived(got, which)

        def open_up(g, _):
            unfolded[pl.ds(pl.multiple_of(g * n, n), n), :] = unfold(got, g)
            return 0

        lax.fori_loop(0, groups, open_up, 0)
        for j in range(mirrors // LO):
            column = pick_b[:, j * LO : (j + 1) * LO]
            group = slot_group[:, j * LO : (j + 1) * LO]
            found = dot(unfolded[pl.ds(0, groups * n), :], column)
            answer = jnp.zeros((n, LO), F32)
            for h in range(groups):
                answer = jnp.where(group == h, found[h * n : (h + 1) * n], answer)
            answer = answer.astype(BF16)
            for c in range(LO // tile):
                b = master_blocks + j * (LO // tile) + c
                local[b, pl.ds(0, n), :] = answer[:, c * tile : (c + 1) * tile]

    def aggregate(n):
        def row_block(i):
            sources = [local[cols_ref[i, k], pl.ds(0, n), :] for k in range(per_row)]
            return dot(jnp.concatenate(sources, axis=1), adj[i], NT)

        def of_masters(i, _):
            own[i, pl.ds(0, n), :] = row_block(i)
            return 0

        def of_mirrors(i, _):
            mirror_part[i - master_blocks, pl.ds(0, n), :] = row_block(i).astype(BF16)
            return 0

        lax.fori_loop(master_blocks, blocks, of_mirrors, 0)
        lax.fori_loop(0, master_blocks, of_masters, 0)

    def give_back(n, box, got, which):
        got[me] = jnp.zeros(got.shape[1:], BF16)
        step = 4
        sums = jnp.concatenate(
            [mirror_part[b, pl.ds(0, n), :] for b in range(mirrors // tile)], axis=1
        )

        def some(d, _):
            first = lax.rem(me // each // step + d, groups // step) * step
            rows = []
            for h in range(step):
                gate = gate_b[first + h]
                rows.append(sums * jnp.concatenate([gate] * (n // 16), axis=0))
            slots = dot(jnp.concatenate(rows, axis=0), pick_b[...], NT)
            for h in range(step):
                fold_and_send(slots[h * n : (h + 1) * n], box, got, which, first + h, n)
            return 0

        lax.fori_loop(0, groups // step, some, 0)

    def combine(n, got, which, mean):
        arrived(got, which)
        size = quarters * n
        total[pl.ds(0, size), :] = jnp.zeros((size, LO), F32)

        def one(g, _):
            values = unfold(got, g)
            rows = []
            for h in range(quarters):
                gate = gate_a[g, h]
                rows.append(values * jnp.concatenate([gate] * (n // 16), axis=0))
            total[pl.ds(0, size), :] += dot(jnp.concatenate(rows, axis=0), pick_a[g], NT)
            return 0

        lax.fori_loop(0, groups, one, 0)
        for b in range(master_blocks):
            h, c = divmod(b * tile, LO)
            sums = own[b, pl.ds(0, n), :] + total[pl.ds(h * n, n), c : c + tile]
            scale = deg_ref[:, b * tile : (b + 1) * tile].astype(F32)
            mean[:, b * tile : (b + 1) * tile] = (sums / scale).astype(BF16)

    def mix(weights, inputs, means):
        count = inputs.shape[0] * inputs.shape[1]
        result = dot(weights[:, :count], inputs[...].reshape(count, masters))
        return result + dot(weights[:, count:], means[...].reshape(count, masters))

    n1, n2 = feat_ref.shape[0], hid.shape[0]
    serve(feat_ref, n1, box_f1, got_f1, 1)

    def take_block(i, _):
        pltpu.make_async_copy(mask_ref.at[i], stage.at[i], mask_sem.at[i]).wait()
        for k in range(per_row):
            adj[i, :, k * tile : (k + 1) * tile] = stage[i, k].astype(F32).astype(BF16)
        return 0

    lax.fori_loop(0, blocks, take_block, 0)
    place(feat_ref, got_f1, 1, n1)
    aggregate(n1)
    give_back(n1, box_r1, got_r1, 2)
    combine(n1, got_r1, 2, agg1)
    share(agg1, agg1_all, 1)
    shared(feat_all, 0)
    shared(agg1_all, 1)
    hid[...] = jnp.maximum(mix(w1, feat_all, agg1_all), 0.0).astype(BF16)

    share(hid, hid_all, 2)
    serve(hid, n2, box_f2, got_f2, 3)
    place(hid, got_f2, 3, n2)
    aggregate(n2)
    give_back(n2, box_r2, got_r2, 4)
    combine(n2, got_r2, 4, agg2)
    share(agg2, agg2_all, 3)
    shared(hid_all, 2)
    shared(agg2_all, 3)
    out_ref[...] = mix(w2, hid_all, agg2_all).astype(BF16)

    sent(want_out, 0)
    for which, box in enumerate((box_f1, box_r1, box_f2, box_r2)):
        sent(box, which + 1)
    for which, everyone in enumerate((feat_all, agg1_all, hid_all, agg2_all)):
        all_sent(everyone, which)


def solution(mesh):
    doms, feats = mesh.shape["dom"], mesh.shape["feat"]

    def on_device(features, tile_mask, tile_cols, replicas, degree, s1, n1, s2, n2):
        rows, masters = features.shape
        mirrors = replicas.shape[1]
        cap = 2 * mirrors // doms
        blocks, per_row, tile, _ = tile_mask.shape
        wide = s1.shape[1] // feats
        groups, quarters = doms * cap // LO, masters // LO
        vmem = pl.BlockSpec(memory_space=pltpu.VMEM)
        box1 = pltpu.VMEM((doms, rows // 2, LANES), BF16)
        box2 = pltpu.VMEM((doms, wide // 2, LANES), BF16)
        dma = pltpu.SemaphoreType.DMA
        scratch = [
            pltpu.VMEM((blocks, per_row, tile, tile), I32),
            pltpu.VMEM((blocks, tile, per_row * tile), BF16),
            pltpu.VMEM((groups, quarters, 16, LO), BF16),
            pltpu.VMEM((groups, LO, LO), BF16),
            pltpu.VMEM((groups, 16, mirrors), BF16),
            pltpu.VMEM((LO, mirrors), BF16),
            pltpu.VMEM((doms, 1, LANES), F32),
            pltpu.VMEM((doms, 1, LANES), F32),
            pltpu.VMEM((groups, 1, LO), I32),
            pltpu.VMEM((wide, 2 * s1.shape[0]), BF16),
            pltpu.VMEM((wide, 2 * s2.shape[0]), BF16),
            pltpu.VMEM((quarters * wide, LO), BF16),
            pltpu.VMEM((groups * wide, LO), BF16),
            pltpu.VMEM((blocks, wide, tile), BF16),
            pltpu.VMEM((masters // tile, wide, tile), F32),
            pltpu.VMEM((mirrors // tile, wide, tile), BF16),
            pltpu.VMEM((quarters * wide, LO), F32),
            pltpu.VMEM((wide, masters), BF16),
            pltpu.VMEM((rows, masters), BF16),
            pltpu.VMEM((wide, masters), BF16),
            pltpu.VMEM((feats, rows, masters), BF16),
            pltpu.VMEM((feats, wide, masters), BF16),
            pltpu.VMEM((feats, rows, masters), BF16),
            pltpu.VMEM((feats, wide, masters), BF16),
            box1, box1, box2, box2, box1, box1, box2, box2,
            dma((blocks,)), dma((5,)), dma((5,)), dma((4,)), dma((4,)),
        ]
        return pl.pallas_call(
            lambda *refs: kernel(doms, feats, cap, *refs),
            name="two_layers",
            out_shape=jax.ShapeDtypeStruct((wide, masters), BF16),
            in_specs=[
                vmem,
                pl.BlockSpec(memory_space=pl.ANY),
                pl.BlockSpec(memory_space=pltpu.SMEM),
                vmem, vmem, vmem, vmem, vmem, vmem,
            ],
            out_specs=vmem,
            scratch_shapes=scratch,
            compiler_params=pltpu.CompilerParams(
                collective_id=0, has_side_effects=True, vmem_limit_bytes=56 << 20
            ),
        )(features, tile_mask, tile_cols, replicas, degree.reshape(1, masters), s1, n1, s2, n2)

    return jax.shard_map(
        on_device,
        mesh=mesh,
        in_specs=(
            P("feat", "dom"),
            P("dom", None, None, None),
            P("dom", None),
            P(None, "dom"),
            P("dom"),
            P(),
            P(),
            P(),
            P(),
        ),
        out_specs=P("feat", "dom"),
        check_vma=False,
    )
```

time: 303 us -> 119 us (0.39)
  Pallas kernels: 0 us -> 116 us
  local copies, waits for them, and re-layouts: 105 us -> 2.93 us
  blocking collectives: 73.1 us -> 0 us
  other arithmetic: 55.8 us -> 0 us
  starting transfers between devices: 35.8 us -> 0 us
  waiting for transfers between devices: 18.8 us -> 0 us
  matrix products: 12.7 us -> 0 us
    pallas_call x0 -> x1, Pallas kernels: none -> 116 us  [on_device(): pl.pallas_call(lambda *refs: kernel(doms, feats, cap, *refs), name='two_l...]
    gather x11 -> x0, local copies, waits for them, and re-layouts: 75.4 us -> none  [the longest x3 24.7 us: combine(): outgoing = jnp.take(padded, send_index, axis=1)]
    scatter-add x2 -> x0, other arithmetic: 48.5 us -> none  [combine(): incoming = jnp.zeros((feature_row_block, masters + 1), jnp.float32).at[:,...]
    all_gather x4 -> x0, blocking collectives: 42.5 us -> none  [the longest x2 21.7 us: mix(): lax.all_gather(inputs, 'feat', axis=0, tiled=True)]
    all_to_all x4 -> x0, starting transfers between devices: 35.8 us -> none  [the longest x1 13.2 us: on_device(): lax.all_to_all(send_rows, 'dom', split_axis=1, concat_axis=1, tiled=True)[0]]
    all_to_all x1 -> x0, blocking collectives: 30.6 us -> none  [on_device(): lax.all_to_all(serve(hidden_master), 'dom', split_axis=1, concat_axis=1,...]
    all_to_all x4 -> x0, waiting for transfers between devices: 18.8 us -> none  [the longest x1 12 us: on_device(): lax.all_to_all(serve(features), 'dom', split_axis=1, concat_axis=1, tiled...]
    unnamed x26 -> x2, local copies, waits for them, and re-layouts: 16.3 us -> 2.93 us
  transfers between devices with their start and end apart: 4 -> 0, of which waited for: 3 -> 0; matrix products, arithmetic and copies ran while one was open for 4% -> 0% of each run, Pallas kernels for 0% -> 0%
where the time goes in v1:
time: 119 us
  Pallas kernels  116 us (97%)
  local copies, waits for them, and re-layouts  2.93 us (2%)
    pallas_call x1, Pallas kernels, on_device(): pl.pallas_call(lambda *refs: kernel(doms, feats, cap, *refs), name='two_l...  116 us
    unnamed x2, local copies, waits for them, and re-layouts  2.93 us

profile of v1, /device:TPU:1, one launch (start us, length us, event | category | flops | bytes accessed | tf_op | source)
XLA Modules:
  0.0 118.5 jit_solution(12726685349980773611)
XLA Ops:
  0.0 1.4 %copy.10.refs_2_ = s32[24,6]{1,0:T(8,128)} copy(s32[24,6]{0,1:T(8,128)} %param.11) | data formatting | bytes 1152 | tf_op args[2]
  1.4 115.6 %two_layers.1 = bf16[64,1024]{1,0:T(8,128)(2,1)} custom-call(bf16[32,1024]{1,0:T(8,128)(2,1)} %refs_0_.1, s32[24,6,128,128]{3,2,1,0:T(8,128)} %refs_1_.1, s32[24,6]{1,0:T(8,128)} %copy.10.refs_2_, s32[3,2048]{1,0:T(4,128)} %refs_3_.1, s32[1,1024]{1,0:T(1,128)} %bitcast.1, bf16[128,256]{1,0:T(8,128)(2,1)} %refs_5_.1, bf16[128,256]{1,0:T(8,128)(2,1)} %refs_6_.1, ...), custom_call_target="tpu_custom_call" | custom-call | tf_op jit(solution)/shard_map/two_layers/pallas_call | solution.py:367
  116.9 1.6 %copy.12 = bf16[64,1024]{1,0:T(8,128)(2,1)} copy(bf16[64,1024]{1,0:T(8,128)(2,1)} %two_layers.1) | data formatting | bytes 262144

commit v2 on v1

--- a/solution.py
+++ b/solution.py
@@ -8,9 +8,19 @@
 F32, BF16, I32 = jnp.float32, jnp.bfloat16, jnp.int32
 MESH = pl.DeviceIdType.MESH
 LANES = 128
+UNROLL_TAKE, UNROLL_READ, UNROLL_SERVE, UNROLL_OPEN, UNROLL_AGG, UNROLL_COMB = 4, 4, 8, 8, 8, 8
 LO = 256
 NN = (((1,), (0,)), ((), ()))
 NT = (((1,), (1,)), ((), ()))
+
+
+def loop(first, last, unroll, body):
+    def some(i, _):
+        for u in range(unroll):
+            body(first + i * unroll + u)
+        return 0
+
+    lax.fori_loop(0, (last - first) // unroll, some, 0)
 
 
 def dot(a, b, dims=NN):
@@ -60,26 +70,20 @@
         rows = lax.broadcasted_iota(I32, (LO, LO), 0)
         hit = rows == slot_column[:, j : j + LO]
         pick_b[:, j : j + LO] = jnp.where(hit, 1.0, 0.0).astype(BF16)
-    for h in range(groups):
-        hit = jnp.where(slot_group == h, 1.0, 0.0)
-        gate_b[h] = jnp.broadcast_to(hit, (16, mirrors)).astype(BF16)
-
     row = reps_ref[2:3, :]
-    kind = lax.broadcasted_iota(I32, (16, 1), 0)
-    words = jnp.where(kind == 0, row & (LO - 1), jnp.where(kind == 1, (row >> 8) + 1, 0))
-    words = words.astype(F32).astype(BF16)
-
-    def name_rows(h, _):
-        slots = dot(words * gate_b[h], pick_b[...], NT)
-        value = slots[1:2] * float(LO) + slots[0:1]
-        for c in range(LO // LANES):
-            pair = value[:, c * LANES : (c + 1) * LANES]
-            swapped = pltpu.roll(pair, cap, 1)
-            want_out[each * h + 2 * c] = jnp.where(low, pair, 0.0)
-            want_out[each * h + 2 * c + 1] = jnp.where(low, swapped, 0.0)
-        return 0
-
-    lax.fori_loop(0, groups, name_rows, 0)
+    here = lax.broadcasted_iota(I32, (groups, mirrors), 0) == slot_group
+    tails = jnp.where(here, row & (LO - 1), 0)
+    heads = jnp.where(here, (row >> 8) + 1, 0)
+    words = jnp.concatenate([tails, heads], axis=0).astype(F32).astype(BF16)
+    slots = dot(words, pick_b[...], NT)
+    slots = slots[groups:] * float(LO) + slots[:groups]
+    for c in range(LO // LANES):
+        pair = slots[:, c * LANES : (c + 1) * LANES]
+        even = jnp.where(low, pair, 0.0)
+        odd = jnp.where(low, pltpu.roll(pair, cap, 1), 0.0)
+        for h in range(groups):
+            want_out[each * h + 2 * c] = even[h : h + 1]
+            want_out[each * h + 2 * c + 1] = odd[h : h + 1]
     want_in[me] = jnp.zeros((1, LANES), F32)
 
     pl.semaphore_wait(barrier, doms - 1 + feats - 1)
@@ -142,9 +146,19 @@
     w2[:, hdim:] = dot(choose, n2_ref[...], NT).astype(BF16)
 
 
+    for h in range(groups):
+        hit = jnp.where(slot_group == h, 1.0, 0.0)
+        gate_b[h] = jnp.broadcast_to(hit, (16, mirrors)).astype(BF16)
+
+    def take_block(i):
+        pltpu.make_async_copy(mask_ref.at[i], stage.at[i], mask_sem.at[i]).wait()
+        for k in range(per_row):
+            adj[i, :, k * tile : (k + 1) * tile] = stage[i, k].astype(F32).astype(BF16)
+
+    loop(0, blocks, UNROLL_TAKE, take_block)
     arrived(want_in, 0)
 
-    def read_wants(g, _):
+    def read_wants(g):
         parts = []
         for c in range(LO // LANES):
             even = want_in[each * g + 2 * c]
@@ -158,11 +172,10 @@
         for h in range(quarters):
             mine = jnp.where(quarter == h + 1, 1.0, 0.0)
             gate_a[g, h] = jnp.broadcast_to(mine, (16, LO)).astype(BF16)
-        return 0
-
-    lax.fori_loop(0, groups, read_wants, 0)
-
-    def fold_and_send(values, box, got, which, g, n):
+
+    loop(0, groups, UNROLL_READ, read_wants)
+
+    def fold(values, box, g, n):
         half = n // 2
         for c in range(LO // LANES):
             pair = values[:, c * LANES : (c + 1) * LANES]
@@ -171,6 +184,8 @@
             odd = pltpu.roll(jnp.where(low, bottom, top), cap, 1)
             box[each * g + 2 * c] = even.astype(BF16)
             box[each * g + 2 * c + 1] = odd.astype(BF16)
+
+    def send_group(box, got, which, g):
         for i in range(each):
             send(box, got, which, each * g + lax.rem(me + i, each))
 
@@ -189,28 +204,32 @@
         for h in range(quarters):
             stacked[pl.ds(h * n, n), :] = values[:, h * LO : (h + 1) * LO]
 
-        def one(d, _):
-            g = lax.rem(me // each + d, groups)
-            found = dot(stacked[pl.ds(0, quarters * n), :], pick_a[g])
-            quarter = whi[g]
-            answer = jnp.zeros((n, LO), F32)
-            for h in range(quarters):
-                answer = jnp.where(quarter == h + 1, found[h * n : (h + 1) * n], answer)
-            fold_and_send(answer, box, got, which, g, n)
+        rows = stacked[pl.ds(0, quarters * n), :]
+
+        def some(d, _):
+            these = [lax.rem(me // each + d * UNROLL_SERVE + u, groups) for u in range(UNROLL_SERVE)]
+            found = [dot(rows, pick_a[g]) for g in these]
+            for g, f in zip(these, found):
+                quarter = whi[g]
+                answer = jnp.zeros((n, LO), F32)
+                for h in range(quarters):
+                    answer = jnp.where(quarter == h + 1, f[h * n : (h + 1) * n], answer)
+                fold(answer, box, g, n)
+            for g in these:
+                send_group(box, got, which, g)
             return 0
 
-        lax.fori_loop(0, groups, one, 0)
+        lax.fori_loop(0, groups // UNROLL_SERVE, some, 0)
 
     def place(values, got, which, n):
         for b in range(master_blocks):
             local[b, pl.ds(0, n), :] = values[:, b * tile : (b + 1) * tile]
         arrived(got, which)
 
-        def open_up(g, _):
+        def open_up(g):
             unfolded[pl.ds(pl.multiple_of(g * n, n), n), :] = unfold(got, g)
-            return 0
-
-        lax.fori_loop(0, groups, open_up, 0)
+
+        loop(0, groups, UNROLL_OPEN, open_up)
         for j in range(mirrors // LO):
             column = pick_b[:, j * LO : (j + 1) * LO]
             group = slot_group[:, j * LO : (j + 1) * LO]
@@ -228,16 +247,20 @@
             sources = [local[cols_ref[i, k], pl.ds(0, n), :] for k in range(per_row)]
             return dot(jnp.concatenate(sources, axis=1), adj[i], NT)
 
-        def of_masters(i, _):
-            own[i, pl.ds(0, n), :] = row_block(i)
+        def of_masters(d, _):
+            these = [d * UNROLL_AGG + u for u in range(UNROLL_AGG)]
+            for i, sums in [(i, row_block(i)) for i in these]:
+                own[i, pl.ds(0, n), :] = sums
             return 0
 
-        def of_mirrors(i, _):
-            mirror_part[i - master_blocks, pl.ds(0, n), :] = row_block(i).astype(BF16)
+        def of_mirrors(d, _):
+            these = [d * UNROLL_AGG + u for u in range(UNROLL_AGG)]
+            for i, sums in [(i, row_block(i + master_blocks)) for i in these]:
+                mirror_part[i, pl.ds(0, n), :] = sums.astype(BF16)
             return 0
 
-        lax.fori_loop(master_blocks, blocks, of_mirrors, 0)
-        lax.fori_loop(0, master_blocks, of_masters, 0)
+        lax.fori_loop(0, (blocks - master_blocks) // UNROLL_AGG, of_mirrors, 0)
+        lax.fori_loop(0, master_blocks // UNROLL_AGG, of_masters, 0)
 
     def give_back(n, box, got, which):
         got[me] = jnp.zeros(got.shape[1:], BF16)
@@ -254,7 +277,9 @@
                 rows.append(sums * jnp.concatenate([gate] * (n // 16), axis=0))
             slots = dot(jnp.concatenate(rows, axis=0), pick_b[...], NT)
             for h in range(step):
-                fold_and_send(slots[h * n : (h + 1) * n], box, got, which, first + h, n)
+                fold(slots[h * n : (h + 1) * n], box, first + h, n)
+            for h in range(step):
+                send_group(box, got, which, first + h)
             return 0
 
         lax.fori_loop(0, groups // step, some, 0)
@@ -264,16 +289,19 @@
         size = quarters * n
         total[pl.ds(0, size), :] = jnp.zeros((size, LO), F32)
 
-        def one(g, _):
-            values = unfold(got, g)
-            rows = []
-            for h in range(quarters):
-                gate = gate_a[g, h]
-                rows.append(values * jnp.concatenate([gate] * (n // 16), axis=0))
-            total[pl.ds(0, size), :] += dot(jnp.concatenate(rows, axis=0), pick_a[g], NT)
+        def some(d, _):
+            sums = []
+            for g in [d * UNROLL_COMB + u for u in range(UNROLL_COMB)]:
+                values = unfold(got, g)
+                rows = []
+                for h in range(quarters):
+                    gate = gate_a[g, h]
+                    rows.append(values * jnp.concatenate([gate] * (n // 16), axis=0))
+                sums.append(dot(jnp.concatenate(rows, axis=0), pick_a[g], NT))
+            total[pl.ds(0, size), :] += sum(sums[1:], sums[0])
             return 0
 
-        lax.fori_loop(0, groups, one, 0)
+        lax.fori_loop(0, groups // UNROLL_COMB, some, 0)
         for b in range(master_blocks):
             h, c = divmod(b * tile, LO)
             sums = own[b, pl.ds(0, n), :] + total[pl.ds(h * n, n), c : c + tile]
@@ -288,13 +316,6 @@
     n1, n2 = feat_ref.shape[0], hid.shape[0]
     serve(feat_ref, n1, box_f1, got_f1, 1)
 
-    def take_block(i, _):
-        pltpu.make_async_copy(mask_ref.at[i], stage.at[i], mask_sem.at[i]).wait()
-        for k in range(per_row):
-            adj[i, :, k * tile : (k + 1) * tile] = stage[i, k].astype(F32).astype(BF16)
-        return 0
-
-    lax.fori_loop(0, blocks, take_block, 0)
     place(feat_ref, got_f1, 1, n1)
     aggregate(n1)
     give_back(n1, box_r1, got_r1, 2)

time: 119 us -> 96.2 us (0.81)
  Pallas kernels: 116 us -> 93.2 us
    pallas_call x1, Pallas kernels: 116 us -> 93.2 us  [on_device(): pl.pallas_call(lambda *refs: kernel(doms, feats, cap, *refs), name='two_l...]
where the time goes in v2:
time: 96.2 us; the launch traced here: 96.1 us
  Pallas kernels  93.2 us (97%)
  local copies, waits for them, and re-layouts  2.93 us (3%)
    pallas_call x1, Pallas kernels, on_device(): pl.pallas_call(lambda *refs: kernel(doms, feats, cap, *refs), name='two_l...  93.2 us
    unnamed x2, local copies, waits for them, and re-layouts  2.93 us

profile of v2, /device:TPU:1, one launch (start us, length us, event | category | flops | bytes accessed | tf_op | source)
XLA Modules:
  0.0 96.1 jit_solution(2532204368461106825)
XLA Ops:
  0.0 1.4 %copy.10.refs_2_ = s32[24,6]{1,0:T(8,128)} copy(s32[24,6]{0,1:T(8,128)} %param.11) | data formatting | bytes 1152 | tf_op args[2]
  1.4 93.2 %two_layers.1 = bf16[64,1024]{1,0:T(8,128)(2,1)} custom-call(bf16[32,1024]{1,0:T(8,128)(2,1)} %refs_0_.1, s32[24,6,128,128]{3,2,1,0:T(8,128)} %refs_1_.1, s32[24,6]{1,0:T(8,128)} %copy.10.refs_2_, s32[3,2048]{1,0:T(4,128)} %refs_3_.1, s32[1,1024]{1,0:T(1,128)} %bitcast.1, bf16[128,256]{1,0:T(8,128)(2,1)} %refs_5_.1, bf16[128,256]{1,0:T(8,128)(2,1)} %refs_6_.1, ...), custom_call_target="tpu_custom_call" | custom-call | tf_op jit(solution)/shard_map/two_layers/pallas_call | solution.py:388
  94.5 1.6 %copy.12 = bf16[64,1024]{1,0:T(8,128)(2,1)} copy(bf16[64,1024]{1,0:T(8,128)(2,1)} %two_layers.1) | data formatting | bytes 262144

commit v3 on v2

--- a/solution.py
+++ b/solution.py
@@ -8,6 +8,7 @@
 F32, BF16, I32 = jnp.float32, jnp.bfloat16, jnp.int32
 MESH = pl.DeviceIdType.MESH
 LANES = 128
+PARTS1, PARTS2 = 2, 2
 UNROLL_TAKE, UNROLL_READ, UNROLL_SERVE, UNROLL_OPEN, UNROLL_AGG, UNROLL_COMB = 4, 4, 8, 8, 8, 8
 LO = 256
 NN = (((1,), (0,)), ((), ()))
@@ -29,16 +30,17 @@
 
 def kernel(
     doms, feats, cap,
-    feat_ref, mask_ref, cols_ref, reps_ref, deg_ref, s1_ref, n1_ref, s2_ref, n2_ref,
+    feat_hbm, mask_ref, cols_ref, reps_ref, deg_hbm, s1_hbm, n1_hbm, s2_hbm, n2_hbm,
     out_ref,
+    feat_ref, deg_ref, s1_ref, n1_ref, s2_ref, n2_ref,
     stage, adj, gate_a, pick_a, gate_b, pick_b, want_out, want_in, whi,
-    w1, w2, stacked, unfolded, local, own, mirror_part,
-    total, hid, agg1, agg2, feat_all, hid_all, agg1_all, agg2_all,
+    w1s, w1n, w2s, w2n, stacked, unfolded, local, own1, own2, mirror_part,
+    total, plain, hid, agg1, agg2, feat_all, hid_all, agg1_all, agg2_all,
     box_f1, box_r1, box_f2, box_r2, got_f1, got_r1, got_f2, got_r2,
-    mask_sem, send_sem, recv_sem, feat_send, feat_recv,
+    in_sem, mask_sem, send_sem, recv_sem, feat_send, feat_recv,
 ):
     me, part = lax.axis_index("dom"), lax.axis_index("feat")
-    blocks, per_row = cols_ref.shape
+    per_row, blocks = cols_ref.shape
     tile = mask_ref.shape[-1]
     masters, mirrors = feat_ref.shape[1], reps_ref.shape[1]
     groups = doms * cap // LO
@@ -47,9 +49,6 @@
     master_blocks = masters // tile
     low = lax.broadcasted_iota(I32, (1, LANES), 1) < cap
 
-    for i in range(blocks):
-        pltpu.make_async_copy(mask_ref.at[i], stage.at[i], mask_sem.at[i]).start()
-
     barrier = pltpu.get_barrier_semaphore()
 
     def greet(d, _):
@@ -63,6 +62,20 @@
         pl.semaphore_signal(
             barrier, 1, device_id={"feat": lax.rem(part + d, feats)}, device_id_type=MESH
         )
+
+    inputs = [
+        pltpu.make_async_copy(source, target, in_sem.at[i])
+        for i, (source, target) in enumerate(
+            (
+                (feat_hbm, feat_ref), (s1_hbm, s1_ref), (n1_hbm, n1_ref),
+                (s2_hbm, s2_ref), (n2_hbm, n2_ref), (deg_hbm, deg_ref),
+            )
+        )
+    ]
+    for copy in inputs:
+        copy.start()
+    for i in range(blocks):
+        pltpu.make_async_copy(mask_ref.at[i], stage.at[i], mask_sem.at[i]).start()
 
     position = reps_ref[0:1, :] * cap + reps_ref[1:2, :]
     slot_group, slot_column = position >> 8, position & (LO - 1)
@@ -133,18 +146,22 @@
         return 0
 
     lax.fori_loop(1, doms, ask, 0)
+    for copy in inputs:
+        copy.wait()
     share(feat_ref, feat_all, 0)
 
-    width = w1.shape[0]
+    width = w1s.shape[0]
     column = lax.broadcasted_iota(I32, (width, s1_ref.shape[1]), 1)
     wanted = lax.broadcasted_iota(I32, column.shape, 0) + part * width
     choose = jnp.where(column == wanted, 1.0, 0.0).astype(BF16)
-    fin, hdim = s1_ref.shape[0], s2_ref.shape[0]
-    w1[:, :fin] = dot(choose, s1_ref[...], NT).astype(BF16)
-    w1[:, fin:] = dot(choose, n1_ref[...], NT).astype(BF16)
-    w2[:, :hdim] = dot(choose, s2_ref[...], NT).astype(BF16)
-    w2[:, hdim:] = dot(choose, n2_ref[...], NT).astype(BF16)
-
+    w1s[...] = dot(choose, s1_ref[...], NT).astype(BF16)
+    w2s[...] = dot(choose, s2_ref[...], NT).astype(BF16)
+    for source, target in ((n1_ref, w1n), (n2_ref, w2n)):
+        mine = source.shape[0] // feats
+        for a in range(target.shape[0]):
+            n = mine // target.shape[0]
+            rows = [source[f * mine + a * n : f * mine + (a + 1) * n] for f in range(feats)]
+            target[a] = dot(choose, jnp.concatenate(rows, axis=0), NT).astype(BF16)
 
     for h in range(groups):
         hit = jnp.where(slot_group == h, 1.0, 0.0)
@@ -200,7 +217,7 @@
         return jnp.concatenate([top, bottom], axis=0).astype(BF16)
 
     def serve(values, n, box, got, which):
-        got[me] = jnp.zeros(got.shape[1:], BF16)
+        got[me] = jnp.zeros((n // 2, LANES), BF16)
         for h in range(quarters):
             stacked[pl.ds(h * n, n), :] = values[:, h * LO : (h + 1) * LO]
 
@@ -242,15 +259,15 @@
                 b = master_blocks + j * (LO // tile) + c
                 local[b, pl.ds(0, n), :] = answer[:, c * tile : (c + 1) * tile]
 
-    def aggregate(n):
+    def aggregate(n, own):
         def row_block(i):
-            sources = [local[cols_ref[i, k], pl.ds(0, n), :] for k in range(per_row)]
+            sources = [local[cols_ref[k, i], pl.ds(0, n), :] for k in range(per_row)]
             return dot(jnp.concatenate(sources, axis=1), adj[i], NT)
 
         def of_masters(d, _):
             these = [d * UNROLL_AGG + u for u in range(UNROLL_AGG)]
             for i, sums in [(i, row_block(i)) for i in these]:
-                own[i, pl.ds(0, n), :] = sums
+                own[i] = sums
             return 0
 
         def of_mirrors(d, _):
@@ -263,7 +280,7 @@
         lax.fori_loop(0, master_blocks // UNROLL_AGG, of_masters, 0)
 
     def give_back(n, box, got, which):
-        got[me] = jnp.zeros(got.shape[1:], BF16)
+        got[me] = jnp.zeros((n // 2, LANES), BF16)
         step = 4
         sums = jnp.concatenate(
             [mirror_part[b, pl.ds(0, n), :] for b in range(mirrors // tile)], axis=1
@@ -284,7 +301,7 @@
 
         lax.fori_loop(0, groups // step, some, 0)
 
-    def combine(n, got, which, mean):
+    def combine(n, own, got, which, mean):
         arrived(got, which)
         size = quarters * n
         total[pl.ds(0, size), :] = jnp.zeros((size, LO), F32)
@@ -304,43 +321,64 @@
         lax.fori_loop(0, groups // UNROLL_COMB, some, 0)
         for b in range(master_blocks):
             h, c = divmod(b * tile, LO)
-            sums = own[b, pl.ds(0, n), :] + total[pl.ds(h * n, n), c : c + tile]
+            sums = own[b] + total[pl.ds(h * n, n), c : c + tile]
             scale = deg_ref[:, b * tile : (b + 1) * tile].astype(F32)
             mean[:, b * tile : (b + 1) * tile] = (sums / scale).astype(BF16)
 
-    def mix(weights, inputs, means):
+    def mix_own(weights, inputs, which):
+        shared(inputs, which)
         count = inputs.shape[0] * inputs.shape[1]
-        result = dot(weights[:, :count], inputs[...].reshape(count, masters))
-        return result + dot(weights[:, count:], means[...].reshape(count, masters))
-
-    n1, n2 = feat_ref.shape[0], hid.shape[0]
-    serve(feat_ref, n1, box_f1, got_f1, 1)
-
-    place(feat_ref, got_f1, 1, n1)
-    aggregate(n1)
-    give_back(n1, box_r1, got_r1, 2)
-    combine(n1, got_r1, 2, agg1)
-    share(agg1, agg1_all, 1)
-    shared(feat_all, 0)
-    shared(agg1_all, 1)
-    hid[...] = jnp.maximum(mix(w1, feat_all, agg1_all), 0.0).astype(BF16)
-
-    share(hid, hid_all, 2)
-    serve(hid, n2, box_f2, got_f2, 3)
-    place(hid, got_f2, 3, n2)
-    aggregate(n2)
-    give_back(n2, box_r2, got_r2, 4)
-    combine(n2, got_r2, 4, agg2)
-    share(agg2, agg2_all, 3)
-    shared(hid_all, 2)
-    shared(agg2_all, 3)
-    out_ref[...] = mix(w2, hid_all, agg2_all).astype(BF16)
+        plain[...] = dot(weights[...], inputs[...].reshape(count, masters))
+
+    def mix_mean(weights, means, first, n):
+        result = plain[first : first + n]
+        for a in range(weights.shape[0]):
+            count = means.shape[1] * means.shape[2]
+            result += dot(weights[a, first : first + n, :], means[a].reshape(count, masters))
+        return result
+
+    def layer(values, weights, inputs, which_in, own, mean, means, which, f, r, first_share):
+        count, n = mean.shape[:2]
+        for a in range(count):
+            place(values[a * n : (a + 1) * n], f[1].at[a], which + a, n)
+            aggregate(n, own.at[a])
+            give_back(n, r[0].at[a], r[1].at[a], which + count + a)
+        mix_own(weights, inputs, which_in)
+        for a in range(count):
+            combine(n, own.at[a], r[1].at[a], which + count + a, mean.at[a])
+            share(mean.at[a], means.at[a], first_share + a)
+        for a in range(count):
+            shared(means.at[a], first_share + a)
+
+    parts1, n1 = agg1.shape[:2]
+    parts2, n2 = agg2.shape[:2]
+    base2, share2 = 1 + 2 * parts1, 2 + parts1
+    boxes1, boxes2 = (box_f1, got_f1), (box_f2, got_f2)
+    back1, back2 = (box_r1, got_r1), (box_r2, got_r2)
+    for a in range(parts1):
+        serve(feat_ref[a * n1 : (a + 1) * n1], n1, box_f1.at[a], got_f1.at[a], 1 + a)
+    layer(feat_ref, w1s, feat_all, 0, own1, agg1, agg1_all, 1, boxes1, back1, 2)
+    for a in range(parts2):
+        rows = jnp.maximum(mix_mean(w1n, agg1_all, a * n2, n2), 0.0).astype(BF16)
+        hid[a * n2 : (a + 1) * n2] = rows
+        serve(hid[a * n2 : (a + 1) * n2], n2, box_f2.at[a], got_f2.at[a], base2 + a)
+    share(hid, hid_all, 1)
+    layer(hid, w2s, hid_all, 1, own2, agg2, agg2_all, base2, boxes2, back2, share2)
+    out_ref[...] = mix_mean(w2n, agg2_all, 0, width).astype(BF16)
 
     sent(want_out, 0)
-    for which, box in enumerate((box_f1, box_r1, box_f2, box_r2)):
-        sent(box, which + 1)
-    for which, everyone in enumerate((feat_all, agg1_all, hid_all, agg2_all)):
-        all_sent(everyone, which)
+    which = 1
+    for box in (box_f1, box_r1, box_f2, box_r2):
+        for a in range(box.shape[0]):
+            sent(box.at[a], which)
+            which += 1
+    all_sent(feat_all, 0)
+    all_sent(hid_all, 1)
+    which = 2
+    for means in (agg1_all, agg2_all):
+        for a in range(means.shape[0]):
+            all_sent(means.at[a], which)
+            which += 1
 
 
 def solution(mesh):
@@ -353,11 +391,18 @@
         blocks, per_row, tile, _ = tile_mask.shape
         wide = s1.shape[1] // feats
         groups, quarters = doms * cap // LO, masters // LO
+        c1, c2 = rows // PARTS1, wide // PARTS2
+        most = max(c1, c2)
         vmem = pl.BlockSpec(memory_space=pltpu.VMEM)
-        box1 = pltpu.VMEM((doms, rows // 2, LANES), BF16)
-        box2 = pltpu.VMEM((doms, wide // 2, LANES), BF16)
+        hbm = pl.BlockSpec(memory_space=pl.ANY)
+        box1 = pltpu.VMEM((PARTS1, doms, c1 // 2, LANES), BF16)
+        box2 = pltpu.VMEM((PARTS2, doms, c2 // 2, LANES), BF16)
         dma = pltpu.SemaphoreType.DMA
+        exchanges, shares = 1 + 2 * (PARTS1 + PARTS2), 2 + PARTS1 + PARTS2
         scratch = [
+            pltpu.VMEM(features.shape, BF16),
+            pltpu.VMEM((1, masters), I32),
+            *(pltpu.VMEM(w.shape, BF16) for w in (s1, n1, s2, n2)),
             pltpu.VMEM((blocks, per_row, tile, tile), I32),
             pltpu.VMEM((blocks, tile, per_row * tile), BF16),
             pltpu.VMEM((groups, quarters, 16, LO), BF16),
@@ -367,40 +412,42 @@
             pltpu.VMEM((doms, 1, LANES), F32),
             pltpu.VMEM((doms, 1, LANES), F32),
             pltpu.VMEM((groups, 1, LO), I32),
-            pltpu.VMEM((wide, 2 * s1.shape[0]), BF16),
-            pltpu.VMEM((wide, 2 * s2.shape[0]), BF16),
-            pltpu.VMEM((quarters * wide, LO), BF16),
-            pltpu.VMEM((groups * wide, LO), BF16),
-            pltpu.VMEM((blocks, wide, tile), BF16),
-            pltpu.VMEM((masters // tile, wide, tile), F32),
-            pltpu.VMEM((mirrors // tile, wide, tile), BF16),
-            pltpu.VMEM((quarters * wide, LO), F32),
+            pltpu.VMEM((wide, s1.shape[0]), BF16),
+            pltpu.VMEM((PARTS1, wide, n1.shape[0] // PARTS1), BF16),
+            pltpu.VMEM((wide, s2.shape[0]), BF16),
+            pltpu.VMEM((PARTS2, wide, n2.shape[0] // PARTS2), BF16),
+            pltpu.VMEM((quarters * most, LO), BF16),
+            pltpu.VMEM((groups * most, LO), BF16),
+            pltpu.VMEM((blocks, most, tile), BF16),
+            pltpu.VMEM((PARTS1, masters // tile, c1, tile), F32),
+            pltpu.VMEM((PARTS2, masters // tile, c2, tile), F32),
+            pltpu.VMEM((mirrors // tile, most, tile), BF16),
+            pltpu.VMEM((quarters * most, LO), F32),
+            pltpu.VMEM((wide, masters), F32),
             pltpu.VMEM((wide, masters), BF16),
-            pltpu.VMEM((rows, masters), BF16),
-            pltpu.VMEM((wide, masters), BF16),
+            pltpu.VMEM((PARTS1, c1, masters), BF16),
+            pltpu.VMEM((PARTS2, c2, masters), BF16),
             pltpu.VMEM((feats, rows, masters), BF16),
             pltpu.VMEM((feats, wide, masters), BF16),
-            pltpu.VMEM((feats, rows, masters), BF16),
-            pltpu.VMEM((feats, wide, masters), BF16),
+            pltpu.VMEM((PARTS1, feats, c1, masters), BF16),
+            pltpu.VMEM((PARTS2, feats, c2, masters), BF16),
             box1, box1, box2, box2, box1, box1, box2, box2,
-            dma((blocks,)), dma((5,)), dma((5,)), dma((4,)), dma((4,)),
+            dma((6,)), dma((blocks,)), dma((exchanges,)), dma((exchanges,)),
+            dma((shares,)), dma((shares,)),
         ]
         return pl.pallas_call(
             lambda *refs: kernel(doms, feats, cap, *refs),
             name="two_layers",
             out_shape=jax.ShapeDtypeStruct((wide, masters), BF16),
             in_specs=[
-                vmem,
-                pl.BlockSpec(memory_space=pl.ANY),
-                pl.BlockSpec(memory_space=pltpu.SMEM),
-                vmem, vmem, vmem, vmem, vmem, vmem,
+                hbm, hbm, pl.BlockSpec(memory_space=pltpu.SMEM), vmem, hbm, hbm, hbm, hbm, hbm,
             ],
             out_specs=vmem,
             scratch_shapes=scratch,
             compiler_params=pltpu.CompilerParams(
                 collective_id=0, has_side_effects=True, vmem_limit_bytes=56 << 20
             ),
-        )(features, tile_mask, tile_cols, replicas, degree.reshape(1, masters), s1, n1, s2, n2)
+        )(features, tile_mask, tile_cols.T, replicas, degree.reshape(1, masters), s1, n1, s2, n2)
 
     return jax.shard_map(
         on_device,

time: 96.2 us -> 86 us (0.89)
  Pallas kernels: 93.2 us -> 84.3 us
  local copies, waits for them, and re-layouts: 2.93 us -> 1.57 us
    pallas_call x1, Pallas kernels: 93.2 us -> 84.3 us  [on_device(): pl.pallas_call(lambda *refs: kernel(doms, feats, cap, *refs), name='two_l...]
    unnamed x2 -> x1, local copies, waits for them, and re-layouts: 2.93 us -> 1.57 us
where the time goes in v3:
time: 86 us; the launch traced here: 85.8 us
  Pallas kernels  84.3 us (98%)
  local copies, waits for them, and re-layouts  1.57 us (2%)
    pallas_call x1, Pallas kernels, on_device(): pl.pallas_call(lambda *refs: kernel(doms, feats, cap, *refs), name='two_l...  84.3 us

profile of v3, /device:TPU:1, one launch (start us, length us, event | category | flops | bytes accessed | tf_op | source)
XLA Modules:
  0.0 85.8 jit_solution(4960268095112081088)
XLA Ops:
  0.0 84.3 %two_layers.1 = bf16[64,1024]{1,0:T(8,128)(2,1)} custom-call(bf16[32,1024]{1,0:T(8,128)(2,1)} %refs_0_.1, s32[24,6,128,128]{3,2,1,0:T(8,128)} %refs_1_.1, s32[6,24]{1,0:T(8,128)} %bitcast.2, s32[3,2048]{1,0:T(4,128)} %refs_3_.1, s32[1,1024]{1,0:T(1,128)} %bitcast.3, bf16[128,256]{1,0:T(8,128)(2,1)} %refs_5_.1, bf16[128,256]{1,0:T(8,128)(2,1)} %refs_6_.1, ...), custom_call_target="tpu_custom_call" | custom-call | tf_op jit(solution)/shard_map/two_layers/pallas_call | solution.py:438
  84.3 1.6 %copy.11 = bf16[64,1024]{1,0:T(8,128)(2,1)} copy(bf16[64,1024]{1,0:T(8,128)(2,1)} %two_layers.1) | data formatting | bytes 262144

commit v4 on v3

--- a/solution.py
+++ b/solution.py
@@ -8,8 +8,8 @@
 F32, BF16, I32 = jnp.float32, jnp.bfloat16, jnp.int32
 MESH = pl.DeviceIdType.MESH
 LANES = 128
-PARTS1, PARTS2 = 2, 2
-UNROLL_TAKE, UNROLL_READ, UNROLL_SERVE, UNROLL_OPEN, UNROLL_AGG, UNROLL_COMB = 4, 4, 8, 8, 8, 8
+TO1, BACK1, TO2, BACK2 = 2, 2, 2, 4
+UNROLL_TAKE, UNROLL_SERVE, UNROLL_OPEN, UNROLL_AGG, UNROLL_COMB = 4, 4, 8, 8, 8
 LO = 256
 NN = (((1,), (0,)), ((), ()))
 NT = (((1,), (1,)), ((), ()))
@@ -33,7 +33,7 @@
     feat_hbm, mask_ref, cols_ref, reps_ref, deg_hbm, s1_hbm, n1_hbm, s2_hbm, n2_hbm,
     out_ref,
     feat_ref, deg_ref, s1_ref, n1_ref, s2_ref, n2_ref,
-    stage, adj, gate_a, pick_a, gate_b, pick_b, want_out, want_in, whi,
+    stage, adj, gate_a, pick_a, gate_b, pick_b, pick_bt, want_out, want_in, whi,
     w1s, w1n, w2s, w2n, stacked, unfolded, local, own1, own2, mirror_part,
     total, plain, hid, agg1, agg2, feat_all, hid_all, agg1_all, agg2_all,
     box_f1, box_r1, box_f2, box_r2, got_f1, got_r1, got_f2, got_r2,
@@ -167,12 +167,9 @@
         hit = jnp.where(slot_group == h, 1.0, 0.0)
         gate_b[h] = jnp.broadcast_to(hit, (16, mirrors)).astype(BF16)
 
-    def take_block(i):
-        pltpu.make_async_copy(mask_ref.at[i], stage.at[i], mask_sem.at[i]).wait()
-        for k in range(per_row):
-            adj[i, :, k * tile : (k + 1) * tile] = stage[i, k].astype(F32).astype(BF16)
-
-    loop(0, blocks, UNROLL_TAKE, take_block)
+    for j in range(0, mirrors, LO):
+        pick_bt[j : j + LO] = jnp.transpose(pick_b[:, j : j + LO].astype(F32)).astype(BF16)
+
     arrived(want_in, 0)
 
     def read_wants(g):
@@ -190,7 +187,6 @@
             mine = jnp.where(quarter == h + 1, 1.0, 0.0)
             gate_a[g, h] = jnp.broadcast_to(mine, (16, LO)).astype(BF16)
 
-    loop(0, groups, UNROLL_READ, read_wants)
 
     def fold(values, box, g, n):
         half = n // 2
@@ -216,7 +212,7 @@
         top, bottom = jnp.concatenate(tops, axis=1), jnp.concatenate(bottoms, axis=1)
         return jnp.concatenate([top, bottom], axis=0).astype(BF16)
 
-    def serve(values, n, box, got, which):
+    def serve(values, n, box, got, which, first=False):
         got[me] = jnp.zeros((n // 2, LANES), BF16)
         for h in range(quarters):
             stacked[pl.ds(h * n, n), :] = values[:, h * LO : (h + 1) * LO]
@@ -225,6 +221,9 @@
 
         def some(d, _):
             these = [lax.rem(me // each + d * UNROLL_SERVE + u, groups) for u in range(UNROLL_SERVE)]
+            if first:
+                for g in these:
+                    read_wants(g)
             found = [dot(rows, pick_a[g]) for g in these]
             for g, f in zip(these, found):
                 quarter = whi[g]
@@ -262,7 +261,7 @@
     def aggregate(n, own):
         def row_block(i):
             sources = [local[cols_ref[k, i], pl.ds(0, n), :] for k in range(per_row)]
-            return dot(jnp.concatenate(sources, axis=1), adj[i], NT)
+            return dot(jnp.concatenate(sources, axis=1), adj[i])
 
         def of_masters(d, _):
             these = [d * UNROLL_AGG + u for u in range(UNROLL_AGG)]
@@ -276,14 +275,16 @@
                 mirror_part[i, pl.ds(0, n), :] = sums.astype(BF16)
             return 0
 
-        lax.fori_loop(0, (blocks - master_blocks) // UNROLL_AGG, of_mirrors, 0)
-        lax.fori_loop(0, master_blocks // UNROLL_AGG, of_masters, 0)
-
-    def give_back(n, box, got, which):
+        if own is None:
+            lax.fori_loop(0, (blocks - master_blocks) // UNROLL_AGG, of_mirrors, 0)
+        else:
+            lax.fori_loop(0, master_blocks // UNROLL_AGG, of_masters, 0)
+
+    def give_back(n, at, box, got, which):
         got[me] = jnp.zeros((n // 2, LANES), BF16)
-        step = 4
+        step = min(groups, LO // 2 // n)
         sums = jnp.concatenate(
-            [mirror_part[b, pl.ds(0, n), :] for b in range(mirrors // tile)], axis=1
+            [mirror_part[b, pl.ds(at, n), :] for b in range(mirrors // tile)], axis=1
         )
 
         def some(d, _):
@@ -292,7 +293,7 @@
             for h in range(step):
                 gate = gate_b[first + h]
                 rows.append(sums * jnp.concatenate([gate] * (n // 16), axis=0))
-            slots = dot(jnp.concatenate(rows, axis=0), pick_b[...], NT)
+            slots = dot(jnp.concatenate(rows, axis=0), pick_bt[...])
             for h in range(step):
                 fold(slots[h * n : (h + 1) * n], box, first + h, n)
             for h in range(step):
@@ -301,7 +302,7 @@
 
         lax.fori_loop(0, groups // step, some, 0)
 
-    def combine(n, own, got, which, mean):
+    def combine(n, own, at, got, which, mean):
         arrived(got, which)
         size = quarters * n
         total[pl.ds(0, size), :] = jnp.zeros((size, LO), F32)
@@ -321,7 +322,7 @@
         lax.fori_loop(0, groups // UNROLL_COMB, some, 0)
         for b in range(master_blocks):
             h, c = divmod(b * tile, LO)
-            sums = own[b] + total[pl.ds(h * n, n), c : c + tile]
+            sums = own[b, pl.ds(at, n), :] + total[pl.ds(h * n, n), c : c + tile]
             scale = deg_ref[:, b * tile : (b + 1) * tile].astype(F32)
             mean[:, b * tile : (b + 1) * tile] = (sums / scale).astype(BF16)
 
@@ -337,28 +338,42 @@
             result += dot(weights[a, first : first + n, :], means[a].reshape(count, masters))
         return result
 
-    def layer(values, weights, inputs, which_in, own, mean, means, which, f, r, first_share):
-        count, n = mean.shape[:2]
+    def layer(values, weights, inputs, which_in, own, mean, means, which, to, back, first_share):
+        count, n = to[1].shape[0], 2 * to[1].shape[2]
+        count_back, n_back = mean.shape[:2]
         for a in range(count):
-            place(values[a * n : (a + 1) * n], f[1].at[a], which + a, n)
+            place(values[a * n : (a + 1) * n], to[1].at[a], which + a, n)
+            aggregate(n, None)
+            for at in range(0, n, n_back):
+                b = (a * n + at) // n_back
+                give_back(n_back, at, back[0].at[b], back[1].at[b], which + count + b)
             aggregate(n, own.at[a])
-            give_back(n, r[0].at[a], r[1].at[a], which + count + a)
         mix_own(weights, inputs, which_in)
-        for a in range(count):
-            combine(n, own.at[a], r[1].at[a], which + count + a, mean.at[a])
-            share(mean.at[a], means.at[a], first_share + a)
-        for a in range(count):
-            shared(means.at[a], first_share + a)
-
-    parts1, n1 = agg1.shape[:2]
-    parts2, n2 = agg2.shape[:2]
-    base2, share2 = 1 + 2 * parts1, 2 + parts1
+        for b in range(count_back):
+            a, at = divmod(b * n_back, n)
+            combine(n_back, own.at[a], at, back[1].at[b], which + count + b, mean.at[b])
+            share(mean.at[b], means.at[b], first_share + b)
+        for b in range(count_back):
+            shared(means.at[b], first_share + b)
+
+    to1, n1 = box_f1.shape[0], 2 * box_f1.shape[2]
+    to2, n2 = box_f2.shape[0], 2 * box_f2.shape[2]
+    base2, share2 = 1 + to1 + agg1.shape[0], 2 + agg1.shape[0]
     boxes1, boxes2 = (box_f1, got_f1), (box_f2, got_f2)
     back1, back2 = (box_r1, got_r1), (box_r2, got_r2)
-    for a in range(parts1):
-        serve(feat_ref[a * n1 : (a + 1) * n1], n1, box_f1.at[a], got_f1.at[a], 1 + a)
+    for a in range(to1):
+        values = feat_ref[a * n1 : (a + 1) * n1]
+        serve(values, n1, box_f1.at[a], got_f1.at[a], 1 + a, a == 0)
+
+    def take_block(i):
+        pltpu.make_async_copy(mask_ref.at[i], stage.at[i], mask_sem.at[i]).wait()
+        for k in range(per_row):
+            entries = stage[i, k].astype(F32)
+            adj[i, k * tile : (k + 1) * tile, :] = jnp.transpose(entries).astype(BF16)
+
+    loop(0, blocks, UNROLL_TAKE, take_block)
     layer(feat_ref, w1s, feat_all, 0, own1, agg1, agg1_all, 1, boxes1, back1, 2)
-    for a in range(parts2):
+    for a in range(to2):
         rows = jnp.maximum(mix_mean(w1n, agg1_all, a * n2, n2), 0.0).astype(BF16)
         hid[a * n2 : (a + 1) * n2] = rows
         serve(hid[a * n2 : (a + 1) * n2], n2, box_f2.at[a], got_f2.at[a], base2 + a)
@@ -391,47 +406,50 @@
         blocks, per_row, tile, _ = tile_mask.shape
         wide = s1.shape[1] // feats
         groups, quarters = doms * cap // LO, masters // LO
-        c1, c2 = rows // PARTS1, wide // PARTS2
-        most = max(c1, c2)
+        t1, t2, b1, b2 = rows // TO1, wide // TO2, rows // BACK1, wide // BACK2
+        most = max(t1, t2)
         vmem = pl.BlockSpec(memory_space=pltpu.VMEM)
         hbm = pl.BlockSpec(memory_space=pl.ANY)
-        box1 = pltpu.VMEM((PARTS1, doms, c1 // 2, LANES), BF16)
-        box2 = pltpu.VMEM((PARTS2, doms, c2 // 2, LANES), BF16)
+        boxes = [
+            pltpu.VMEM((count, doms, n // 2, LANES), BF16)
+            for count, n in ((TO1, t1), (BACK1, b1), (TO2, t2), (BACK2, b2))
+        ]
         dma = pltpu.SemaphoreType.DMA
-        exchanges, shares = 1 + 2 * (PARTS1 + PARTS2), 2 + PARTS1 + PARTS2
+        exchanges, shares = 1 + TO1 + BACK1 + TO2 + BACK2, 2 + BACK1 + BACK2
         scratch = [
             pltpu.VMEM(features.shape, BF16),
             pltpu.VMEM((1, masters), I32),
             *(pltpu.VMEM(w.shape, BF16) for w in (s1, n1, s2, n2)),
             pltpu.VMEM((blocks, per_row, tile, tile), I32),
-            pltpu.VMEM((blocks, tile, per_row * tile), BF16),
+            pltpu.VMEM((blocks, per_row * tile, tile), BF16),
             pltpu.VMEM((groups, quarters, 16, LO), BF16),
             pltpu.VMEM((groups, LO, LO), BF16),
             pltpu.VMEM((groups, 16, mirrors), BF16),
             pltpu.VMEM((LO, mirrors), BF16),
+            pltpu.VMEM((mirrors, LO), BF16),
             pltpu.VMEM((doms, 1, LANES), F32),
             pltpu.VMEM((doms, 1, LANES), F32),
             pltpu.VMEM((groups, 1, LO), I32),
             pltpu.VMEM((wide, s1.shape[0]), BF16),
-            pltpu.VMEM((PARTS1, wide, n1.shape[0] // PARTS1), BF16),
+            pltpu.VMEM((BACK1, wide, n1.shape[0] // BACK1), BF16),
             pltpu.VMEM((wide, s2.shape[0]), BF16),
-            pltpu.VMEM((PARTS2, wide, n2.shape[0] // PARTS2), BF16),
+            pltpu.VMEM((BACK2, wide, n2.shape[0] // BACK2), BF16),
             pltpu.VMEM((quarters * most, LO), BF16),
             pltpu.VMEM((groups * most, LO), BF16),
             pltpu.VMEM((blocks, most, tile), BF16),
-            pltpu.VMEM((PARTS1, masters // tile, c1, tile), F32),
-            pltpu.VMEM((PARTS2, masters // tile, c2, tile), F32),
+            pltpu.VMEM((TO1, masters // tile, t1, tile), F32),
+            pltpu.VMEM((TO2, masters // tile, t2, tile), F32),
             pltpu.VMEM((mirrors // tile, most, tile), BF16),
             pltpu.VMEM((quarters * most, LO), F32),
             pltpu.VMEM((wide, masters), F32),
             pltpu.VMEM((wide, masters), BF16),
-            pltpu.VMEM((PARTS1, c1, masters), BF16),
-            pltpu.VMEM((PARTS2, c2, masters), BF16),
+            pltpu.VMEM((BACK1, b1, masters), BF16),
+            pltpu.VMEM((BACK2, b2, masters), BF16),
             pltpu.VMEM((feats, rows, masters), BF16),
             pltpu.VMEM((feats, wide, masters), BF16),
-            pltpu.VMEM((PARTS1, feats, c1, masters), BF16),
-            pltpu.VMEM((PARTS2, feats, c2, masters), BF16),
-            box1, box1, box2, box2, box1, box1, box2, box2,
+            pltpu.VMEM((BACK1, feats, b1, masters), BF16),
+            pltpu.VMEM((BACK2, feats, b2, masters), BF16),
+            *boxes, *boxes,
             dma((6,)), dma((blocks,)), dma((exchanges,)), dma((exchanges,)),
             dma((shares,)), dma((shares,)),
         ]

time: 86 us -> 80.6 us (0.937)
  Pallas kernels: 84.3 us -> 78.8 us
    pallas_call x1, Pallas kernels: 84.3 us -> 78.8 us  [on_device(): pl.pallas_call(lambda *refs: kernel(doms, feats, cap, *refs), name='two_l...]
where the time goes in v4:
time: 80.6 us; the launch traced here: 80.4 us
  Pallas kernels  78.8 us (98%)
  local copies, waits for them, and re-layouts  1.57 us (2%)
    pallas_call x1, Pallas kernels, on_device(): pl.pallas_call(lambda *refs: kernel(doms, feats, cap, *refs), name='two_l...  78.8 us

profile of v4, /device:TPU:1, one launch (start us, length us, event | category | flops | bytes accessed | tf_op | source)
XLA Modules:
  0.0 80.4 jit_solution(1380332326957426862)
XLA Ops:
  0.0 78.8 %two_layers.1 = bf16[64,1024]{1,0:T(8,128)(2,1)} custom-call(bf16[32,1024]{1,0:T(8,128)(2,1)} %refs_0_.1, s32[24,6,128,128]{3,2,1,0:T(8,128)} %refs_1_.1, s32[6,24]{1,0:T(8,128)} %bitcast.2, s32[3,2048]{1,0:T(4,128)} %refs_3_.1, s32[1,1024]{1,0:T(1,128)} %bitcast.3, bf16[128,256]{1,0:T(8,128)(2,1)} %refs_5_.1, bf16[128,256]{1,0:T(8,128)(2,1)} %refs_6_.1, ...), custom_call_target="tpu_custom_call" | custom-call | tf_op jit(solution)/shard_map/two_layers/pallas_call | solution.py:456
  78.9 1.6 %copy.11 = bf16[64,1024]{1,0:T(8,128)(2,1)} copy(bf16[64,1024]{1,0:T(8,128)(2,1)} %two_layers.1) | data formatting | bytes 262144

commit v5 on v4

--- a/solution.py
+++ b/solution.py
@@ -74,8 +74,6 @@
     ]
     for copy in inputs:
         copy.start()
-    for i in range(blocks):
-        pltpu.make_async_copy(mask_ref.at[i], stage.at[i], mask_sem.at[i]).start()
 
     position = reps_ref[0:1, :] * cap + reps_ref[1:2, :]
     slot_group, slot_column = position >> 8, position & (LO - 1)
@@ -146,6 +144,8 @@
         return 0
 
     lax.fori_loop(1, doms, ask, 0)
+    for i in range(blocks):
+        pltpu.make_async_copy(mask_ref.at[i], stage.at[i], mask_sem.at[i]).start()
     for copy in inputs:
         copy.wait()
     share(feat_ref, feat_all, 0)
@@ -282,7 +282,7 @@
 
     def give_back(n, at, box, got, which):
         got[me] = jnp.zeros((n // 2, LANES), BF16)
-        step = min(groups, LO // 2 // n)
+        step = min(groups, LO // n)
         sums = jnp.concatenate(
             [mirror_part[b, pl.ds(at, n), :] for b in range(mirrors // tile)], axis=1
         )

time: 80.6 us -> 79.8 us (0.990)
  no operation moved by 1% of the time
where the time goes in v5:
time: 79.8 us; the launch traced here: 79.7 us
  Pallas kernels  78.1 us (98%)
  local copies, waits for them, and re-layouts  1.57 us (2%)
    pallas_call x1, Pallas kernels, on_device(): pl.pallas_call(lambda *refs: kernel(doms, feats, cap, *refs), name='two_l...  78.1 us

profile of v5, /device:TPU:1, one launch (start us, length us, event | category | flops | bytes accessed | tf_op | source)
XLA Modules:
  0.0 79.7 jit_solution(40068293230921287)
XLA Ops:
  0.0 78.1 %two_layers.1 = bf16[64,1024]{1,0:T(8,128)(2,1)} custom-call(bf16[32,1024]{1,0:T(8,128)(2,1)} %refs_0_.1, s32[24,6,128,128]{3,2,1,0:T(8,128)} %refs_1_.1, s32[6,24]{1,0:T(8,128)} %bitcast.2, s32[3,2048]{1,0:T(4,128)} %refs_3_.1, s32[1,1024]{1,0:T(1,128)} %bitcast.3, bf16[128,256]{1,0:T(8,128)(2,1)} %refs_5_.1, bf16[128,256]{1,0:T(8,128)(2,1)} %refs_6_.1, ...), custom_call_target="tpu_custom_call" | custom-call | tf_op jit(solution)/shard_map/two_layers/pallas_call | solution.py:456
  78.1 1.6 %copy.11 = bf16[64,1024]{1,0:T(8,128)(2,1)} copy(bf16[64,1024]{1,0:T(8,128)(2,1)} %two_layers.1) | data formatting | bytes 262144

commit v6 on v5

--- a/solution.py
+++ b/solution.py
@@ -72,8 +72,7 @@
             )
         )
     ]
-    for copy in inputs:
-        copy.start()
+    inputs[0].start()
 
     position = reps_ref[0:1, :] * cap + reps_ref[1:2, :]
     slot_group, slot_column = position >> 8, position & (LO - 1)
@@ -144,11 +143,14 @@
         return 0
 
     lax.fori_loop(1, doms, ask, 0)
+    for copy in inputs[1:]:
+        copy.start()
     for i in range(blocks):
         pltpu.make_async_copy(mask_ref.at[i], stage.at[i], mask_sem.at[i]).start()
-    for copy in inputs:
+    inputs[0].wait()
+    share(feat_ref, feat_all, 0)
+    for copy in inputs[1:]:
         copy.wait()
-    share(feat_ref, feat_all, 0)
 
     width = w1s.shape[0]
     column = lax.broadcasted_iota(I32, (width, s1_ref.shape[1]), 1)

time: 79.8 us -> 79.8 us (level)
  no operation moved by 1% of the time
where the time goes in v6:
time: 79.8 us; the launch traced here: 79.6 us
  Pallas kernels  78 us (98%)
  local copies, waits for them, and re-layouts  1.57 us (2%)
    pallas_call x1, Pallas kernels, on_device(): pl.pallas_call(lambda *refs: kernel(doms, feats, cap, *refs), name='two_l...  78 us

profile of v6, /device:TPU:1, one launch (start us, length us, event | category | flops | bytes accessed | tf_op | source)
XLA Modules:
  0.0 79.6 jit_solution(10097630004609989675)
XLA Ops:
  0.0 78.0 %two_layers.1 = bf16[64,1024]{1,0:T(8,128)(2,1)} custom-call(bf16[32,1024]{1,0:T(8,128)(2,1)} %refs_0_.1, s32[24,6,128,128]{3,2,1,0:T(8,128)} %refs_1_.1, s32[6,24]{1,0:T(8,128)} %bitcast.2, s32[3,2048]{1,0:T(4,128)} %refs_3_.1, s32[1,1024]{1,0:T(1,128)} %bitcast.3, bf16[128,256]{1,0:T(8,128)(2,1)} %refs_5_.1, bf16[128,256]{1,0:T(8,128)(2,1)} %refs_6_.1, ...), custom_call_target="tpu_custom_call" | custom-call | tf_op jit(solution)/shard_map/two_layers/pallas_call | solution.py:458
  78.0 1.6 %copy.11 = bf16[64,1024]{1,0:T(8,128)(2,1)} copy(bf16[64,1024]{1,0:T(8,128)(2,1)} %two_layers.1) | data formatting | bytes 262144
